TPU v7x, 512 devices: a whole 4x4x16 slice. The times are simulated.
512 devices in a mesh: blk: 8 (over z_lo), stripe: 64 (over y, x, z_hi, core).
Axes of the slice: x: 4, y: 4, z: 16 (z_hi: 2, z_lo: 8; z = z_hi * 8 + z_lo), core: 2. Of those that a mesh axis runs over, the one named last changes fastest.
Arguments:
- points: bfloat16 [262144, 64], P(('blk', 'stripe')), may hold values from -6 to 6
- coefficients: float32 [262144], P(('blk', 'stripe')), may hold values from -0.0234375 to 0.0234375
- velocity: float32 [262144], P(('blk', 'stripe')), may hold values from -0.0234375 to 0.0234375
- targets: float32 [262144], P(('blk', 'stripe')), may hold values from -6 to 6
- batch_rows: int32 [32768], P(('blk', 'stripe')), may hold values from 0 to 511
- counts: int32 [8, 64], P('blk', 'stripe'), may hold values from 1 to 64, 2048 in all within a row
Outputs:
- new_coefficients: float32 [262144], P(('blk', 'stripe'))
- new_velocity: float32 [262144], P(('blk', 'stripe'))
Inputs may be any that keep to these rules, and one draw needn't show every extreme that they name: In every index of blk, the counts of its 64 devices sum to exactly 2048, and some device's count is exactly 64. Only the first count entries of a device's slots are live. `batch_rows`: every entry, live or not, indexes the points of the device that holds it; rows may repeat.
All inputs are finite; a program needn't handle non-finite values.
Results may differ from a plain program's by a relative error of at most 0.0003.
Values may be sent and summed in bfloat16 or wider, within the bound.
A program may use at most 64 MiB of HBM per device.

v0:
```python
import math
import jax
import jax.numpy as jnp
from jax import lax
from jax.sharding import PartitionSpec as P

MOMENTUM = 0.9
STEP_SIZE = 1.0
NOISE_VAR = 8.0
KERNEL_RATE = 3.0**0.5 / 6.0


def matern_sums(row_feats, row_sq, col_points, col_coef):
    col_sq = jnp.sum(jnp.square(col_points.astype(jnp.float32)), axis=1)
    inner_prod = lax.dot_general(
        row_feats, col_points, (((1,), (1,)), ((), ())), preferred_element_type=jnp.float32
    )
    distance = jnp.sqrt(jnp.maximum(row_sq[:, None] + col_sq[None, :] - 2.0 * inner_prod, 0.0))
    scaled = KERNEL_RATE * distance
    kernel_tile = (1.0 + scaled) * jnp.exp(-scaled)
    return jnp.sum(kernel_tile * col_coef[None, :], axis=1)


def column_sums(row_feats, points, preview):
    row_sq = jnp.sum(jnp.square(row_feats.astype(jnp.float32)), axis=1)
    every_coef = lax.all_gather(preview, "blk", axis=0, tiled=True)
    zeros_init = jnp.zeros((row_feats.shape[0],), jnp.float32)
    piece_points = lax.all_gather(points, "blk", axis=0, tiled=True)
    piece_len = piece_points.shape[0]
    block_len = math.gcd(piece_len, 512)
    point_blocks = piece_points.reshape(-1, block_len, piece_points.shape[1])
    coef_blocks = every_coef.reshape(-1, block_len)

    def advance(partial_sum, column_block):
        return (
            partial_sum + matern_sums(row_feats, row_sq, column_block[0], column_block[1]),
            None,
        )

    result, unused = lax.scan(advance, zeros_init, (point_blocks, coef_blocks))
    return result


def per_device(points, coefficients, velocity, targets, batch_rows, counts):
    preview = coefficients + MOMENTUM * velocity
    slot_total = batch_rows.shape[0]
    local_size = points.shape[0]
    slot_ids = jnp.arange(slot_total, dtype=jnp.int32)
    count_here = counts.reshape((1,))
    in_count = slot_ids < count_here[0]
    picked = jnp.take(points, batch_rows, axis=0)
    group_rows = lax.all_gather(picked, "stripe", axis=0, tiled=True)
    partial_value = column_sums(group_rows, points, preview)
    kernel_rows = lax.psum_scatter(partial_value, "stripe", scatter_dimension=0, tiled=True)
    residual = jnp.where(
        in_count,
        kernel_rows + NOISE_VAR * jnp.take(preview, batch_rows) - jnp.take(targets, batch_rows),
        0.0,
    )
    scatter_rows = (batch_rows[:, None] == jnp.arange(local_size, dtype=jnp.int32)[None, :]).astype(
        jnp.float32
    )
    update_sum = jnp.dot(residual, scatter_rows, precision=lax.Precision.HIGHEST)
    new_velocity = MOMENTUM * velocity - STEP_SIZE * update_sum
    new_coefficients = coefficients + new_velocity
    return (new_coefficients, new_velocity)


def solution(mesh):
    in_specs = (
        P(("blk", "stripe"), None),
        P(("blk", "stripe")),
        P(("blk", "stripe")),
        P(("blk", "stripe")),
        P(("blk", "stripe")),
        P("blk", "stripe"),
    )
    out_specs = (P(("blk", "stripe")), P(("blk", "stripe")))
    return jax.shard_map(
        per_device, mesh=mesh, in_specs=in_specs, out_specs=out_specs, check_vma=False
    )
```

profile of v0, /device:TPU:0, one launch (start us, length us, event | category | flops | bytes accessed | tf_op | source)
XLA Modules:
  0.0 868.9 jit_solution(8727007130608261097)
XLA Ops:
  0.6 0.0 copy-start
  0.6 0.0 copy-start.1
  1.3 1.3 dynamic-slice
  3.3 0.7 compare_and_fusion
  3.9 0.7 compare_select_fusion
  4.6 0.7 multiply_add_fusion
  5.3 0.0 copy-done
  5.3 0.8 gather_fusion.2
  6.1 0.8 gather_fusion.1
  6.9 42.5 %all-gather = f32[8,1,512]{2,1,0:T(1,128)S(1)} all-gather(f32[1,1,512]{2,1,0:T(1,128)S(1)} %bitcast.38), channel_id=1, replica_groups=mesh['blk'=8,'stripe'=64] {'blk'}, dimensions={0}, use_global_device_ids=true | all-gather | bytes 18432 | tf_op jit(solution)/shard_map/all_gather | solution.py:26
  49.4 0.0 copy-done.1
  49.4 0.1 copy.12
  49.6 0.6 gather_fusion
  50.2 0.1 broadcast_select_fusion
  50.3 48.0 %all_gather.10 = bf16[4096,64]{0,1:T(8,128)(2,1)S(1)} all-gather(bf16[512,64]{0,1:T(8,128)(2,1)S(1)} %copy-done.1), channel_id=1, replica_groups=mesh['blk'=8,'stripe'=64] {'blk'}, dimensions={0}, use_global_device_ids=true | all-gather | bytes 589824 | tf_op jit(solution)/shard_map/all_gather | solution.py:28
  98.3 0.5 copy.13
  98.8 165.0 %all_gather.9 = bf16[4096,64]{1,0:T(8,128)(2,1)S(1)} all-gather(bf16[64,64]{1,0:T(8,128)(2,1)S(1)} %broadcast_select_fusion), channel_id=1, replica_groups=mesh['blk'=8,'stripe'=64] {'stripe'}, dimensions={0}, use_global_device_ids=true | all-gather | bytes 532480 | tf_op jit(solution)/shard_map/all_gather | solution.py:52
  263.8 0.6 multiply_reduce_fusion.2
  264.5 0.0 copy-start.4
  264.5 0.0 copy-start.2
  264.5 0.0 copy-start.3
  264.5 49.6 %while.11 = (s32[]{:T(128)}, f32[4096]{0:T(1024)S(1)}, f32[4096]{0:T(1024)S(1)}, bf16[8,512,64]{2,1,0:T(8,128)(2,1)S(1)}, bf16[4096,64]{1,0:T(8,128)(2,1)S(1)}, /*index=5*/f32[8,512]{1,0:T(8,128)S(1)}, s32[]{:T(128)}, s32[]{:T(128)}) while((s32[]{:T(128)}, f32[4096]{0:T(1024)S(1)}, f32[4096]{0:T(1024)S(1)}, ...), condition=%wide.region_4.5_spmd.clone, body=%wide.region_1.0_spmd.clone.sunk | while | flops 289508864 | bytes 1337459 | solution.py:40
  264.5 0.2 multiply_reduce_fusion.5
  264.7 6.0 multiply_reduce_fusion.6
  270.7 0.2 multiply_reduce_fusion.5
  270.9 6.0 multiply_reduce_fusion.6
  276.9 0.2 multiply_reduce_fusion.5
  277.1 6.0 multiply_reduce_fusion.6
  283.1 0.2 multiply_reduce_fusion.5
  283.3 6.0 multiply_reduce_fusion.6
  289.3 0.2 multiply_reduce_fusion.5
  289.5 6.0 multiply_reduce_fusion.6
  295.5 0.2 multiply_reduce_fusion.5
  295.7 6.0 multiply_reduce_fusion.6
  301.7 0.2 multiply_reduce_fusion.5
  301.9 6.0 multiply_reduce_fusion.6
  307.9 0.2 multiply_reduce_fusion.5
  308.1 6.0 multiply_reduce_fusion.6
  314.1 554.0 %all-reduce = f32[4096]{0:T(1024)S(1)} all-reduce(f32[4096]{0:T(1024)S(1)} %get-tuple-element.35), channel_id=2, replica_groups=mesh['blk'=8,'stripe'=64] {'stripe'}, use_global_device_ids=true, to_apply=%region_5.6.clone | all-reduce | flops 4096 | bytes 32768
  868.1 0.0 copy-done.4
  868.1 0.2 fusion.6
  868.3 0.0 copy-done.2
  868.3 0.0 copy-done.3
  868.3 0.6 fusion.21
  (19 shorter events, 0.1 us)
Async XLA Ops:
  0.6 4.7 copy-start
  0.6 48.8 %copy-start.1 = (bf16[512,64]{0,1:T(8,128)(2,1)S(1)}, bf16[512,64]{0,1:T(8,128)(2,1)}, u32[]{:S(2)}) copy-start(bf16[512,64]{0,1:T(8,128)(2,1)} %param.10) | copy-start | bytes 196612
  264.5 603.6 %copy-start.4 = (s32[64]{0:T(128)S(1)}, s32[64]{0:T(128)}, u32[]{:S(2)}) copy-start(s32[64]{0:T(128)} %param.14) | copy-start | bytes 772
  264.5 603.9 %copy-start.2 = (f32[512]{0:T(512)S(1)}, f32[512]{0:T(512)}, u32[]{:S(2)}) copy-start(f32[512]{0:T(512)} %param.11) | copy-start | bytes 6148
  264.5 603.8 %copy-start.3 = (f32[512]{0:T(512)S(1)}, f32[512]{0:T(512)}, u32[]{:S(2)}) copy-start(f32[512]{0:T(512)} %param.12) | copy-start | bytes 6148
where the time goes:
time: 869 us
  blocking collectives  810 us (93%)
  matrix products  48.1 us (6%)
    unnamed x1, blocking collectives  554 us
    all_gather x1, blocking collectives, per_device(): group_rows = lax.all_gather(picked, 'stripe', axis=0, tiled=True)  165 us
    all_gather x1, blocking collectives, column_sums(): piece_points = lax.all_gather(points, 'blk', axis=0, tiled=True)  48 us
    dot_general x8, matrix products, matern_sums(): lax.dot_general(row_feats, col_points, (((1,), (1,)), ((), ())), preferre...  47.9 us
    all_gather x1, blocking collectives, column_sums(): every_coef = lax.all_gather(preview, 'blk', axis=0, tiled=True)  42.5 us

commit v1 on v0

--- a/solution.py
+++ b/solution.py
@@ -8,6 +8,13 @@
 STEP_SIZE = 1.0
 NOISE_VAR = 8.0
 KERNEL_RATE = 3.0**0.5 / 6.0
+
+
+def all_by_exchange(value, name, d):
+    devices = lax.axis_size(name)
+    tiles = jnp.stack([value for _ in range(devices)])
+    tiles = lax.all_to_all(tiles, name, split_axis=0, concat_axis=0)
+    return jnp.concatenate(tiles, axis=d)
 
 
 def matern_sums(row_feats, row_sq, col_points, col_coef):
@@ -23,7 +30,7 @@
 
 def column_sums(row_feats, points, preview):
     row_sq = jnp.sum(jnp.square(row_feats.astype(jnp.float32)), axis=1)
-    every_coef = lax.all_gather(preview, "blk", axis=0, tiled=True)
+    every_coef = all_by_exchange(preview, "blk", 0)
     zeros_init = jnp.zeros((row_feats.shape[0],), jnp.float32)
     piece_points = lax.all_gather(points, "blk", axis=0, tiled=True)
     piece_len = piece_points.shape[0]

time: 869 us -> 838 us (0.964)
  blocking collectives: 810 us -> 766 us
    all_gather x1 -> x0, blocking collectives: 42.5 us -> none  [column_sums(): every_coef = lax.all_gather(preview, 'blk', axis=0, tiled=True)]
  transfers between devices with their start and end apart: 0 -> 1, of which waited for: 0 -> 0; matrix products, arithmetic and copies ran while one was open for 0% -> 1% of each run, Pallas kernels for 0% -> 0%
where the time goes in v1:
time: 838 us; the launch traced here: 834 us
  blocking collectives  766 us (91%)
  matrix products  48.2 us (6%)
    unnamed x1, blocking collectives  556 us
    all_gather x1, blocking collectives, per_device(): group_rows = lax.all_gather(picked, 'stripe', axis=0, tiled=True)  162 us
    all_gather x1, blocking collectives, column_sums(): piece_points = lax.all_gather(points, 'blk', axis=0, tiled=True)  48.5 us
    dot_general x8, matrix products, matern_sums(): lax.dot_general(row_feats, col_points, (((1,), (1,)), ((), ())), preferre...  48 us
  transfers between devices with their start and end apart: 1, of which 0 were waited for; matrix products, arithmetic and copies ran while one was open for 1% of the time, Pallas kernels for 0%

profile of v1, /device:TPU:0, one launch (start us, length us, event | category | flops | bytes accessed | tf_op | source)
XLA Modules:
  0.0 834.4 jit_solution(18284601904768405946)
XLA Ops:
  0.6 0.0 copy-start
  0.6 0.7 multiply_add_fusion
  1.4 0.6 stack.2
  2.0 7.2 all-to-all-start
  9.1 0.7 compare_and_fusion
  9.8 0.7 compare_select_fusion
  10.4 1.0 copy.12
  11.4 48.5 %all_gather.7 = bf16[4096,64]{0,1:T(8,128)(2,1)S(1)} all-gather(bf16[512,64]{0,1:T(8,128)(2,1)} %param.10), channel_id=1, replica_groups=mesh['blk'=8,'stripe'=64] {'blk'}, dimensions={0}, use_global_device_ids=true | all-gather | bytes 589824 | tf_op jit(solution)/shard_map/all_gather | solution.py:35
  59.9 0.6 gather_fusion
  60.5 0.1 broadcast_select_fusion
  60.6 162.0 %all_gather.6 = bf16[4096,64]{1,0:T(8,128)(2,1)S(1)} all-gather(bf16[64,64]{1,0:T(8,128)(2,1)S(1)} %broadcast_select_fusion), channel_id=1, replica_groups=mesh['blk'=8,'stripe'=64] {'stripe'}, dimensions={0}, use_global_device_ids=true | all-gather | bytes 532480 | tf_op jit(solution)/shard_map/all_gather | solution.py:59
  222.5 0.6 multiply_reduce_fusion.2
  223.2 0.8 gather_fusion.1
  224.6 0.0 copy-done
  224.6 0.8 gather_fusion.2
  225.4 0.5 copy.13
  225.9 1.3 dynamic-slice
  227.8 0.0 all-to-all-done
  227.9 0.0 copy-start.3
  227.9 0.0 copy-start.1
  227.9 0.0 copy-start.2
  227.9 49.7 %while.11 = (s32[]{:T(128)}, f32[4096]{0:T(1024)S(1)}, f32[4096]{0:T(1024)S(1)}, bf16[8,512,64]{2,1,0:T(8,128)(2,1)S(1)}, bf16[4096,64]{1,0:T(8,128)(2,1)S(1)}, /*index=5*/f32[8,512]{1,0:T(8,128)S(1)}, s32[]{:T(128)}, s32[]{:T(128)}) while((s32[]{:T(128)}, f32[4096]{0:T(1024)S(1)}, f32[4096]{0:T(1024)S(1)}, ...), condition=%wide.region_4.5_spmd.clone, body=%wide.region_1.0_spmd.clone.sunk | while | flops 289508864 | bytes 1337459 | solution.py:47
  227.9 0.2 multiply_reduce_fusion.5
  228.1 6.0 multiply_reduce_fusion.6
  234.1 0.2 multiply_reduce_fusion.5
  234.3 6.0 multiply_reduce_fusion.6
  240.3 0.2 multiply_reduce_fusion.5
  240.5 6.0 multiply_reduce_fusion.6
  246.5 0.2 multiply_reduce_fusion.5
  246.7 6.0 multiply_reduce_fusion.6
  252.8 0.2 multiply_reduce_fusion.5
  252.9 6.0 multiply_reduce_fusion.6
  259.0 0.2 multiply_reduce_fusion.5
  259.1 6.0 multiply_reduce_fusion.6
  265.2 0.2 multiply_reduce_fusion.5
  265.3 6.0 multiply_reduce_fusion.6
  271.4 0.2 multiply_reduce_fusion.5
  271.5 6.0 multiply_reduce_fusion.6
  277.6 556.0 %all-reduce = f32[4096]{0:T(1024)S(1)} all-reduce(f32[4096]{0:T(1024)S(1)} %get-tuple-element.35), channel_id=2, replica_groups=mesh['blk'=8,'stripe'=64] {'stripe'}, use_global_device_ids=true, to_apply=%region_5.6.clone | all-reduce | flops 4096 | bytes 32768
  833.5 0.0 copy-done.3
  833.5 0.2 fusion.6
  833.8 0.0 copy-done.1
  833.8 0.0 copy-done.2
  833.8 0.6 fusion.21
  (19 shorter events, 0.1 us)
Async XLA Ops:
  0.6 224.0 %copy-start = (f32[512]{0:T(512)S(1)}, f32[512]{0:T(512)}, u32[]{:S(2)}) copy-start(f32[512]{0:T(512)} %param.13) | copy-start | bytes 6148
  2.0 225.9 %all-to-all-start = ((f32[8,1,512]{2,1,0:T(1,128)}), f32[8,1,512]{2,1,0:T(1,128)S(1)}, u32[]{:S(2)}, u32[]{:S(2)}) async-start(f32[8,1,512]{2,1,0:T(1,128)} %stack.2), calls=%async_computation | async-start | bytes 32768 | tf_op jit(solution)/shard_map/all_to_all | solution.py:16
  227.9 605.7 %copy-start.3 = (s32[64]{0:T(128)S(1)}, s32[64]{0:T(128)}, u32[]{:S(2)}) copy-start(s32[64]{0:T(128)} %param.14) | copy-start | bytes 772
  227.9 605.9 %copy-start.1 = (f32[512]{0:T(512)S(1)}, f32[512]{0:T(512)}, u32[]{:S(2)}) copy-start(f32[512]{0:T(512)} %param.11) | copy-start | bytes 6148
  227.9 605.9 %copy-start.2 = (f32[512]{0:T(512)S(1)}, f32[512]{0:T(512)}, u32[]{:S(2)}) copy-start(f32[512]{0:T(512)} %param.12) | copy-start | bytes 6148
